TPU v7x, 128 devices: a whole 4x4x4 slice. The times are simulated.
128 devices in a mesh: seq: 16 (over y, x), exp: 8 (over z, core).
Axes of the slice: x: 4, y: 4, z: 4, core: 2. Of those that a mesh axis runs over, the one named last changes fastest.
Arguments:
- queries: bfloat16 [2048, 8192], P('seq', 'exp'), may hold values from -0.5 to 0.5
- keys: bfloat16 [2048, 8192], P('seq', 'exp'), may hold values from -0.5 to 0.5
- values: bfloat16 [2048, 8192], P('seq', 'exp'), may hold values from -6 to 6
- attn_grad: bfloat16 [2048, 8192], P('seq', 'exp'), may hold values from -6 to 6
- log_decay: float32 [2048, 64], P('seq', 'exp'), may hold values from -0.75 to 0, as said below
- moe_grad: bfloat16 [2048, 6144], P('seq', 'exp'), may hold values from -6 to 6
- gate_probs: bfloat16 [2048, 2], P('seq'), may hold values from 0.099609375 to 0.8984375
- expert_ids: int32 [2048, 2], P('seq'), may hold values from 0 to 7, all different within a row; in each aligned block of 128 rows (0 to 127, 128 to 255, ...) at most 48 rows name the same one
- hidden_acts: bfloat16 [8, 768, 9216], P('exp', None, 'seq'), may hold values from -0.3125 to 0.3125
- down_weight: bfloat16 [8, 9216, 6144], P('exp', 'seq'), may hold values from -0.0625 to 0.0625
Outputs:
- query_grad: bfloat16 [2048, 8192], P('seq', 'exp')
- key_grad: bfloat16 [2048, 8192], P('seq', 'exp')
- value_grad: bfloat16 [2048, 8192], P('seq', 'exp')
- hidden_grad: bfloat16 [8, 768, 9216], P('exp', None, 'seq')
- weight_grad: bfloat16 [8, 9216, 6144], P('exp', 'seq')
- gate_grad: float32 [2048, 2], P('seq')
Inputs may be any that keep to these rules, and one draw needn't show every extreme that they name: `expert_ids`: each row names 2 different experts. In the 128 rows of one index of seq no expert is named by more than 48 rows, and every draw has such a block where some expert is named by exactly 48 rows. `log_decay`: log decay of each head at each position; never positive.
All inputs are finite; a program needn't handle non-finite values.
Results may differ from a plain program's by a relative error of at most 0.005.
Values may be sent and summed in bfloat16 or wider, within the bound.
A program may use at most 128 MiB of HBM per device.

v0:
```python
import jax
import jax.numpy as jnp
from jax import lax
from jax.sharding import PartitionSpec as P

precise = lax.Precision.HIGHEST


def prefix(part, axis, combine, identity, reverse):
    count = lax.axis_size(axis)
    place = lax.axis_index(axis)
    ahead = count - 1 - place if reverse else place
    gathered = jax.tree.map(lambda a: lax.all_gather(a, axis), part)
    state = jax.tree.map(lambda a, e: jnp.zeros_like(a) + jnp.asarray(e, a.dtype), part, identity)

    def one(lap, state):
        source = count - 1 - lap if reverse else lap
        return combine(
            state, jax.tree.map(lambda a: lax.dynamic_index_in_dim(a, source, 0, False), gathered)
        )

    return lax.fori_loop(0, ahead, one, state)


def chain_combine(earlier, latter):
    return (jnp.exp(latter[1])[:, None, None] * earlier[0] + latter[0], earlier[1] + latter[1])


def on_device(
    queries,
    keys,
    values,
    attn_grad,
    log_decay,
    moe_grad,
    gate_probs,
    expert_ids,
    hidden_acts,
    down_weight,
):
    tok_count = queries.shape[0]
    head_count = log_decay.shape[1]
    head_width = queries.shape[1] // head_count
    shaped = (tok_count, head_count, head_width)
    query_f = queries.astype(jnp.float32).reshape(shaped)
    key_f = keys.astype(jnp.float32).reshape(shaped)
    value_f = values.astype(jnp.float32).reshape(shaped)
    grad_f = attn_grad.astype(jnp.float32).reshape(shaped)
    cumul = jnp.cumsum(log_decay, axis=0)
    total = cumul[-1]
    tail_w = jnp.exp(total[None, :] - cumul)
    lead_w = jnp.exp(cumul)
    state_kv = jnp.einsum("th,thi,thj->hij", tail_w, key_f, value_f, precision=precise)
    state_qg = jnp.einsum("th,thi,thj->hij", lead_w, query_f, grad_f, precision=precise)
    zero_state = jnp.zeros_like(state_kv)
    zero_gain = jnp.zeros_like(total)
    incoming = prefix((state_kv, total), "seq", chain_combine, (zero_state, zero_gain), False)[0]
    upcoming = prefix((state_qg, total), "seq", chain_combine, (zero_state, zero_gain), True)[0]
    causal = jnp.arange(tok_count)[:, None] >= jnp.arange(tok_count)[None, :]
    spread = cumul.T[:, :, None] - cumul.T[:, None, :]
    decay_mask = jnp.exp(jnp.where(causal[None], spread, -jnp.inf))
    grad_scores = jnp.einsum("thj,shj->hts", grad_f, value_f, precision=precise) * decay_mask
    qk_scores = jnp.einsum("thi,shi->hts", query_f, key_f, precision=precise) * decay_mask
    query_g = jnp.einsum("hts,shi->thi", grad_scores, key_f, precision=precise)
    query_g = query_g + lead_w[:, :, None] * jnp.einsum(
        "thj,hij->thi", grad_f, incoming, precision=precise
    )
    key_g = jnp.einsum("hts,thi->shi", grad_scores, query_f, precision=precise)
    key_g = key_g + tail_w[:, :, None] * jnp.einsum(
        "shj,hij->shi", value_f, upcoming, precision=precise
    )
    value_g = jnp.einsum("hts,thj->shj", qk_scores, grad_f, precision=precise)
    value_g = value_g + tail_w[:, :, None] * jnp.einsum(
        "shi,hij->shj", key_f, upcoming, precision=precise
    )
    flat_width = head_count * head_width
    query_grad = query_g.reshape(tok_count, flat_width).astype(jnp.bfloat16)
    key_grad = key_g.reshape(tok_count, flat_width).astype(jnp.bfloat16)
    value_grad = value_g.reshape(tok_count, flat_width).astype(jnp.bfloat16)
    expert_here = lax.axis_index("exp")
    cap_size = hidden_acts.shape[1] // lax.axis_size("seq")
    chosen_here = expert_ids == expert_here
    routed = jnp.any(chosen_here, axis=1)
    token_gate = jnp.sum(jnp.where(chosen_here, gate_probs.astype(jnp.float32), 0.0), axis=1)
    slot_rank = jnp.cumsum(routed.astype(jnp.int32)) - 1
    slot_ids = jnp.arange(cap_size, dtype=jnp.int32)
    selector = ((slot_rank[None, :] == slot_ids[:, None]) & routed[None, :]).astype(jnp.float32)
    slot_gate = jnp.dot(selector, token_gate, precision=precise).astype(jnp.bfloat16)
    whole_rows = lax.all_gather(moe_grad, "exp", axis=1, tiled=True)
    slot_rows = jnp.dot(
        selector.astype(jnp.bfloat16), whole_rows, preferred_element_type=jnp.float32
    ).astype(jnp.bfloat16)
    weight_here = down_weight[0]
    hidden_here = hidden_acts[0]
    piece_rows = lax.all_gather(slot_rows, "seq", axis=0, tiled=True)
    piece_gate = lax.all_gather(slot_gate, "seq", axis=0, tiled=True)
    back_rows = lax.dot_general(
        piece_rows, weight_here, (((1,), (1,)), ((), ())), preferred_element_type=jnp.float32
    )
    gate_col = piece_gate.astype(jnp.float32)[:, None]
    hidden_out = (gate_col * back_rows).astype(jnp.bfloat16)
    piece_parts = jnp.sum(back_rows * hidden_here.astype(jnp.float32), axis=1)
    slot_parts = piece_parts
    weighted = (gate_col * piece_rows.astype(jnp.float32)).astype(jnp.bfloat16)
    grad_sum = lax.dot_general(
        hidden_here, weighted, (((0,), (0,)), ((), ())), preferred_element_type=jnp.float32
    )
    grad_sum, hidden_out, slot_parts = (grad_sum, hidden_out, slot_parts)
    own_parts = lax.psum_scatter(slot_parts, "seq", scatter_dimension=0, tiled=True)
    per_token = jnp.dot(selector.T, own_parts, precision=precise)
    local_gate = jnp.where(chosen_here, per_token[:, None], 0.0)
    gate_grad = lax.psum(local_gate, "exp")
    return (
        query_grad,
        key_grad,
        value_grad,
        hidden_out[None],
        grad_sum.astype(jnp.bfloat16)[None],
        gate_grad,
    )


def solution(mesh):
    return jax.shard_map(
        on_device,
        mesh=mesh,
        in_specs=(
            P("seq", "exp"),
            P("seq", "exp"),
            P("seq", "exp"),
            P("seq", "exp"),
            P("seq", "exp"),
            P("seq", "exp"),
            P("seq", None),
            P("seq", None),
            P("exp", None, "seq"),
            P("exp", "seq", None),
        ),
        out_specs=(
            P("seq", "exp"),
            P("seq", "exp"),
            P("seq", "exp"),
            P("exp", None, "seq"),
            P("exp", "seq", None),
            P("seq", None),
        ),
        check_vma=False,
    )
```

profile of v0, /device:TPU:1, one launch (start us, length us, event | category | flops | bytes accessed | tf_op | source)
XLA Modules:
  0.0 343.7 jit_solution(9725436786065418335)
XLA Ops:
  7.2 0.0 copy-start
  7.2 0.0 copy-start.1
  7.2 0.0 all-gather.8.cloned.1.call-start
  7.2 0.7 all-gather.8.cloned.1.call-update
  7.9 0.0 all-gather.12.cloned.1.call-start
  8.0 0.8 copy.64
  8.8 1.1 copy.67
  9.9 0.2 reduce_window_sum.18
  10.1 0.0 copy-done
  10.2 1.2 fusion.21
  11.4 0.0 all-gather.12.cloned.1.call-update
  11.4 0.0 all-gather.14.cloned.1.call-start
  11.4 1.1 copy.93
  12.6 1.1 copy.74
  13.8 1.5 fusion.18
  15.2 0.0 all-gather.14.cloned.1.call-update
  15.3 0.0 all-gather.10.cloned.1.call-start
  15.3 0.7 select_reduce_fusion
  16.1 0.1 copy.83
  16.2 0.2 reduce-window.8
  16.4 0.1 add_reduce_fusion
  16.5 21.5 %all-gather.8.cloned.1.call-done = bf16[128,6144]{1,0:T(8,128)(2,1)} async-done(((bf16[128,768]{1,0:T(8,128)(2,1)}), bf16[128,6144]{1,0:T(8,128)(2,1)}) %all-gather.8.cloned.1.call-update) | async-done | bytes 1572880 | tf_op jit(solution)/shard_map/all_gather | solution.py:89
  37.9 2.6 convolution_convert_fusion
  40.5 0.0 all-gather.10.cloned.1.call-update
  40.6 0.6 fusion.44
  41.8 0.1 fusion.15
  41.9 0.2 dynamic-update-slice
  42.1 33.4 %all-reduce = bf16[768]{0:T(1024)(128)(2,1)S(1)} all-reduce(bf16[768]{0:T(1024)(128)(2,1)S(1)} %dynamic-update-slice), channel_id=1, replica_groups=mesh['seq'=16,'exp'=8] {'seq'}, use_global_device_ids=true, to_apply=%add | all-reduce | flops 768 | bytes 3072
  76.2 15.0 %all-gather.2 = f32[16,1,8]{2,1,0:T(1,128)S(1)} all-gather(f32[1,1,8]{2,1,0:T(1,128)S(1)} %get-tuple-element.211), channel_id=1, replica_groups=mesh['seq'=16,'exp'=8] {'seq'}, dimensions={0}, use_global_device_ids=true | all-gather | bytes 544 | tf_op jit(solution)/shard_map/all_gather | solution.py:13
  91.2 0.3 convolution_multiply_fusion.1
  91.5 0.3 convolution_multiply_fusion
  91.9 19.4 %all-gather.12.cloned.1.call-done = f32[128,128,128]{2,1,0:T(8,128)} async-done(((f32[8,128,128]{2,1,0:T(8,128)}), f32[128,128,128]{2,1,0:T(8,128)}) %all-gather.12.cloned.1.call-update) | async-done | bytes 8388624 | tf_op jit(solution)/shard_map/all_gather | solution.py:13
  111.3 0.4 fusion.7
  111.7 0.7 fusion.14
  112.4 0.8 copy.84
  113.2 70.5 %all-gather.14.cloned.1.call-done = f32[128,128,128]{2,1,0:T(8,128)} async-done(((f32[8,128,128]{2,1,0:T(8,128)}), f32[128,128,128]{2,1,0:T(8,128)}) %all-gather.14.cloned.1.call-update) | async-done | bytes 8388624 | tf_op jit(solution)/shard_map/all_gather | solution.py:13
  183.7 18.6 %while.27 = (s32[]{:T(128)}, f32[8,128,128]{2,1,0:T(8,128)S(1)}, s32[]{:T(128)}, f32[16,8]{1,0:T(8,128)S(1)}, f32[16,8,128,128]{3,2,1,0:T(8,128)}, /*index=5*/s32[]{:T(128)}, s32[]{:T(128)}, s32[]{:T(128)}, s32[]{:T(128)}) while((s32[]{:T(128)}, f32[8,128,128]{2,1,0:T(8,128)S(1)}, s32[]{:T(128)}, f32[16,8]{1,0:T(8,128)S(1)}, ...), condition=%wide.region_4.5_spmd, body=%wide.region_3.4_spmd.sunk | while | flops 262150 | bytes 1573115 | solution.py:22
  183.8 1.2 bitcast_add_fusion.5
  185.0 1.2 bitcast_add_fusion.5
  186.2 1.2 bitcast_add_fusion.5
  187.5 1.2 bitcast_add_fusion.5
  188.7 1.2 bitcast_add_fusion.5
  189.9 1.2 bitcast_add_fusion.5
  191.2 1.2 bitcast_add_fusion.5
  192.4 1.2 bitcast_add_fusion.5
  193.6 1.2 bitcast_add_fusion.5
  194.9 1.2 bitcast_add_fusion.5
  196.1 1.2 bitcast_add_fusion.5
  197.4 1.2 bitcast_add_fusion.5
  198.6 1.2 bitcast_add_fusion.5
  199.9 1.2 bitcast_add_fusion.5
  201.1 1.2 bitcast_add_fusion.5
  202.3 0.7 fusion.9
  203.0 0.4 fusion.13
  203.4 0.8 copy.85
  204.2 0.6 fusion.11
  204.8 0.4 fusion.12
  205.2 0.9 copy.86
  206.1 55.5 %all-gather.10.cloned.1.call-done = bf16[768,6144]{1,0:T(8,128)(2,1)} async-done(((bf16[48,6144]{1,0:T(8,128)(2,1)}), bf16[768,6144]{1,0:T(8,128)(2,1)}) %all-gather.10.cloned.1.call-update) | async-done | bytes 9437200 | tf_op jit(solution)/shard_map/all_gather | solution.py:95
  261.6 11.6 %multiply_reduce_fusion = (f32[768]{0:T(1024)S(1)}, bf16[1,768,576]{1,2,0:T(8,128)(2,1)}) fusion(bf16[1,768,576]{1,2,0:T(8,128)(2,1)} %param.22, f32[768]{0:T(1024)S(1)} %convert_element_type.83, bf16[768,6144]{1,0:T(8,128)(2,1)} %all-gather.10.cloned.1.call-done, bf16[1,576,6144]{2,1,0:T(8,128)(2,1)} %param.23), kind=kOutput, calls=%fused_computation.12 | convolution fusion | flops 5438028800 | bytes 18290688 | tf_op jit(solution)/shard_map/dot_general | solution.py:97
  273.2 31.2 %all-reduce.1 = f32[768]{0:T(1024)S(1)} all-reduce(f32[768]{0:T(1024)S(1)} %get-tuple-element.206), channel_id=4, replica_groups=mesh['seq'=16,'exp'=8] {'seq'}, use_global_device_ids=true, to_apply=%region_9.10.clone | all-reduce | flops 768 | bytes 6144
  304.3 0.2 convolution_bitcast_fusion.6
  304.5 20.6 %psum.7 = f32[128,2]{0,1:T(2,128)} all-reduce(f32[128,2]{0,1:T(2,128)S(1)} %broadcast_select_fusion), channel_id=1, replica_groups=mesh['seq'=16,'exp'=8] {'exp'}, use_global_device_ids=true, to_apply=%region_10.11 | all-reduce | flops 256 | bytes 2048 | tf_op jit(solution)/shard_map/psum | solution.py:112
  325.1 12.0 %fusion.3 = bf16[1,576,6144]{2,1,0:T(8,128)(2,1)} fusion(bf16[768,6144]{1,0:T(8,128)(2,1)} %all-gather.10.cloned.1.call-done, f32[768]{0:T(1024)S(1)} %convert_element_type.83, bf16[1,768,576]{1,2,0:T(8,128)(2,1)S(1)} %copy-done.2), kind=kOutput, calls=%fused_computation.8 | convolution fusion | flops 5453512704 | bytes 17402880 | tf_op jit(solution)/shard_map/dot_general | solution.py:105
  (32 shorter events, 0.5 us)
Async XLA Ops:
  7.2 3.0 copy-start
  7.2 33.4 %copy-start.1 = (u32[128]{0:T(128)S(1)}, u32[128]{0:T(128)}, u32[]{:S(2)}) copy-start(u32[128]{0:T(128)} %constant.81) | copy-start | bytes 1540
  7.2 30.7 %all-gather.8.cloned.1.call-start = ((), (), s32[]{:S(2)}) async-start(), calls=%async_computation | async-start | bytes 1769472 | tf_op jit(solution)/shard_map/all_gather | solution.py:89
  7.9 103.3 %all-gather.12.cloned.1.call-start = ((), (), s32[]{:S(2)}) async-start(), calls=%async_computation.2 | async-start | bytes 8912896 | tf_op jit(solution)/shard_map/all_gather | solution.py:13
  11.4 172.3 %all-gather.14.cloned.1.call-start = ((), (), s32[]{:S(2)}) async-start(), calls=%async_computation.3 | async-start | bytes 8912896 | tf_op jit(solution)/shard_map/all_gather | solution.py:13
  15.3 246.3 %all-gather.10.cloned.1.call-start = ((), (), s32[]{:S(2)}) async-start(), calls=%async_computation.1 | async-start | bytes 10027008 | tf_op jit(solution)/shard_map/all_gather | solution.py:95
  206.1 119.0 %copy-start.2 = (bf16[1,768,576]{1,2,0:T(8,128)(2,1)S(1)}, bf16[1,768,576]{1,2,0:T(8,128)(2,1)}, u32[]{:S(2)}) copy-start(bf16[1,768,576]{1,2,0:T(8,128)(2,1)} %param.22) | copy-start | bytes 2654212
Sparse Core Ops, SparseCore 0:
  9.7 28.1 all-gather.7
  40.6 70.5 all-gather.11
  113.4 70.2 all-gather.13
  186.2 75.2 all-gather.9
where the time goes:
time: 345 us; the launch traced here: 344 us
  waiting for transfers between devices  168 us (49%)
  blocking collectives  100 us (29%)
  matrix products  33 us (10%)
  other arithmetic  19.2 us (6%)
  between operations  15.2 us (4%)
  local copies, waits for them, and re-layouts  8.11 us (2%)
    all_gather x2, waiting for transfers between devices, prefix(): gathered = jax.tree.map(lambda a: lax.all_gather(a, axis), part)  89.8 us
    unnamed x2, blocking collectives  64.5 us
    all_gather x1, waiting for transfers between devices, on_device(): piece_rows = lax.all_gather(slot_rows, 'seq', axis=0, tiled=True)  55.5 us
    all_gather x1, waiting for transfers between devices, on_device(): whole_rows = lax.all_gather(moe_grad, 'exp', axis=1, tiled=True)  21.5 us
    psum x1, blocking collectives, on_device(): gate_grad = lax.psum(local_gate, 'exp')  20.6 us
    add x15, other arithmetic, chain_combine(): jnp.exp(latter[1])[:, None, None] * earlier[0] + latter[0]  17.9 us
    all_gather x1, blocking collectives, prefix(): gathered = jax.tree.map(lambda a: lax.all_gather(a, axis), part)  15 us
    dot_general x1, matrix products, on_device(): lax.dot_general(hidden_here, weighted, (((0,), (0,)), ((), ())), preferre...  12 us
  transfers between devices with their start and end apart: 4, of which 4 were waited for; matrix products, arithmetic and copies ran while one was open for 11% of the time, Pallas kernels for 0%

commit v1 on v0

--- a/solution.py
+++ b/solution.py
@@ -86,7 +86,9 @@
     slot_ids = jnp.arange(cap_size, dtype=jnp.int32)
     selector = ((slot_rank[None, :] == slot_ids[:, None]) & routed[None, :]).astype(jnp.float32)
     slot_gate = jnp.dot(selector, token_gate, precision=precise).astype(jnp.bfloat16)
-    whole_rows = lax.all_gather(moe_grad, "exp", axis=1, tiled=True)
+    whole_rows = jnp.concatenate(
+        lax.all_to_all(jnp.stack([moe_grad] * lax.axis_size("exp")), "exp", 0, 0), axis=1
+    )
     slot_rows = jnp.dot(
         selector.astype(jnp.bfloat16), whole_rows, preferred_element_type=jnp.float32
     ).astype(jnp.bfloat16)

time: 345 us -> 319 us (0.925)
  waiting for transfers between devices: 168 us -> 135 us
  starting transfers between devices: 0.16 us -> 6.9 us
    all_gather x2, waiting for transfers between devices: 89.8 us -> 59.6 us  [prefix(): gathered = jax.tree.map(lambda a: lax.all_gather(a, axis), part)]
    all_gather x1 -> x0, waiting for transfers between devices: 21.5 us -> none  [on_device(): whole_rows = lax.all_gather(moe_grad, 'exp', axis=1, tiled=True)]
    all_to_all x0 -> x1, waiting for transfers between devices: none -> 20.3 us  [on_device(): lax.all_to_all(jnp.stack([moe_grad] * lax.axis_size('exp')), 'exp', 0, 0)]
    all_to_all x0 -> x1, starting transfers between devices: none -> 6.81 us  [on_device(): lax.all_to_all(jnp.stack([moe_grad] * lax.axis_size('exp')), 'exp', 0, 0)]
    unnamed x15 -> x20, local copies, waits for them, and re-layouts: 6.47 us -> 7.59 us
  transfers between devices with their start and end apart: 4 -> 4, of which waited for: 4 -> 3; matrix products, arithmetic and copies ran while one was open for 11% -> 11% of each run, Pallas kernels for 0% -> 0%
where the time goes in v1:
time: 319 us; the launch traced here: 318 us
  waiting for transfers between devices  135 us (42%)
  blocking collectives  98.9 us (31%)
  matrix products  31.8 us (10%)
  other arithmetic  18.5 us (6%)
  between operations  15.3 us (5%)
  local copies, waits for them, and re-layouts  10.6 us (3%)
  starting transfers between devices  6.9 us (2%)
    unnamed x2, blocking collectives  65.4 us
    all_gather x2, waiting for transfers between devices, prefix(): gathered = jax.tree.map(lambda a: lax.all_gather(a, axis), part)  59.6 us
    all_gather x1, waiting for transfers between devices, on_device(): piece_rows = lax.all_gather(slot_rows, 'seq', axis=0, tiled=True)  55.6 us
    psum x1, blocking collectives, on_device(): gate_grad = lax.psum(local_gate, 'exp')  20.6 us
    all_to_all x1, waiting for transfers between devices, on_device(): lax.all_to_all(jnp.stack([moe_grad] * lax.axis_size('exp')), 'exp', 0, 0)  20.3 us
    add x15, other arithmetic, chain_combine(): jnp.exp(latter[1])[:, None, None] * earlier[0] + latter[0]  18 us
    all_gather x1, blocking collectives, prefix(): gathered = jax.tree.map(lambda a: lax.all_gather(a, axis), part)  13 us
    dot_general x1, matrix products, on_device(): lax.dot_general(hidden_here, weighted, (((0,), (0,)), ((), ())), preferre...  11.9 us
  transfers between devices with their start and end apart: 4, of which 3 were waited for; matrix products, arithmetic and copies ran while one was open for 11% of the time, Pallas kernels for 0%

profile of v1, /device:TPU:1, one launch (start us, length us, event | category | flops | bytes accessed | tf_op | source)
XLA Modules:
  0.0 317.9 jit_solution(10792344098132005387)
XLA Ops:
  7.2 0.0 copy-start
  7.2 0.0 copy-start.1
  7.2 0.0 copy-start.3
  7.2 0.0 copy-start.2
  7.2 0.0 all-gather.9.cloned.1.call-start
  7.3 0.8 copy.65
  8.1 0.2 reduce_window_sum.18
  8.3 1.1 copy.68
  9.5 1.2 fusion.21
  10.7 0.0 all-gather.9.cloned.1.call-update
  10.7 0.0 all-gather.11.cloned.1.call-start
  10.8 1.1 copy.95
  11.9 1.1 copy.75
  13.1 1.5 fusion.18
  14.6 0.0 all-gather.11.cloned.1.call-update
  14.6 1.1 copy.85
  15.7 1.4 stack.2
  17.0 6.8 %all-to-all-start = ((bf16[8,128,768]{1,2,0:T(8,128)(2,1)}), bf16[8,128,768]{1,2,0:T(8,128)(2,1)S(1)}, u32[]{:S(2)}, u32[]{:S(2)}) async-start(bf16[8,128,768]{1,2,0:T(8,128)(2,1)} %stack.2), calls=%async_computation | async-start | bytes 3145728 | tf_op jit(solution)/shard_map/all_to_all | solution.py:90
  23.9 0.1 copy.84
  24.0 0.2 reduce-window.8
  24.2 0.1 add_reduce_fusion
  24.3 20.3 %all-to-all-done = bf16[8,128,768]{1,2,0:T(8,128)(2,1)S(1)} async-done(((bf16[8,128,768]{1,2,0:T(8,128)(2,1)}), bf16[8,128,768]{1,2,0:T(8,128)(2,1)S(1)}, u32[]{:S(2)}, u32[]{:S(2)}) %all-to-all-start) | async-done | bytes 1572896 | tf_op jit(solution)/shard_map/all_to_all | solution.py:90
  44.5 1.5 convolution_convert_fusion
  46.0 0.0 all-gather.7.cloned.1.call-update
  46.1 0.6 fusion.44
  47.4 0.1 fusion.15
  47.5 0.2 dynamic-update-slice
  47.7 34.2 %all-reduce = bf16[768]{0:T(1024)(128)(2,1)S(1)} all-reduce(bf16[768]{0:T(1024)(128)(2,1)S(1)} %dynamic-update-slice), channel_id=1, replica_groups=mesh['seq'=16,'exp'=8] {'seq'}, use_global_device_ids=true, to_apply=%add | all-reduce | flops 768 | bytes 3072
  82.6 13.0 %all-gather.2 = f32[16,1,8]{2,1,0:T(1,128)S(1)} all-gather(f32[1,1,8]{2,1,0:T(1,128)S(1)} %get-tuple-element.211), channel_id=1, replica_groups=mesh['seq'=16,'exp'=8] {'seq'}, dimensions={0}, use_global_device_ids=true | all-gather | bytes 544 | tf_op jit(solution)/shard_map/all_gather | solution.py:13
  95.6 0.3 convolution_multiply_fusion.1
  95.9 0.3 convolution_multiply_fusion
  96.3 0.0 all-gather.9.cloned.1.call-done
  96.4 0.4 fusion.7
  96.8 0.7 fusion.14
  97.4 0.9 copy.86
  98.3 59.5 %all-gather.11.cloned.1.call-done = f32[128,128,128]{2,1,0:T(8,128)} async-done(((f32[8,128,128]{2,1,0:T(8,128)}), f32[128,128,128]{2,1,0:T(8,128)}) %all-gather.11.cloned.1.call-update) | async-done | bytes 8388624 | tf_op jit(solution)/shard_map/all_gather | solution.py:13
  157.9 18.6 %while.27 = (s32[]{:T(128)}, f32[8,128,128]{2,1,0:T(8,128)S(1)}, s32[]{:T(128)}, f32[16,8]{1,0:T(8,128)S(1)}, f32[16,8,128,128]{3,2,1,0:T(8,128)}, /*index=5*/s32[]{:T(128)}, s32[]{:T(128)}, s32[]{:T(128)}, s32[]{:T(128)}) while((s32[]{:T(128)}, f32[8,128,128]{2,1,0:T(8,128)S(1)}, s32[]{:T(128)}, f32[16,8]{1,0:T(8,128)S(1)}, ...), condition=%wide.region_4.5_spmd, body=%wide.region_3.4_spmd.sunk | while | flops 262150 | bytes 1573115 | solution.py:22
  157.9 1.2 bitcast_add_fusion.5
  159.1 1.2 bitcast_add_fusion.5
  160.4 1.2 bitcast_add_fusion.5
  161.6 1.2 bitcast_add_fusion.5
  162.8 1.2 bitcast_add_fusion.5
  164.1 1.2 bitcast_add_fusion.5
  165.3 1.2 bitcast_add_fusion.5
  166.5 1.2 bitcast_add_fusion.5
  167.8 1.2 bitcast_add_fusion.5
  169.0 1.2 bitcast_add_fusion.5
  170.3 1.2 bitcast_add_fusion.5
  171.5 1.2 bitcast_add_fusion.5
  172.8 1.2 bitcast_add_fusion.5
  174.0 1.2 bitcast_add_fusion.5
  175.3 1.2 bitcast_add_fusion.5
  176.5 0.7 fusion.9
  177.2 0.4 fusion.13
  177.6 0.9 copy.87
  178.4 0.6 fusion.11
  179.0 0.4 fusion.12
  179.5 0.9 copy.88
  180.3 55.6 %all-gather.7.cloned.1.call-done = bf16[768,6144]{1,0:T(8,128)(2,1)} async-done(((bf16[48,6144]{1,0:T(8,128)(2,1)}), bf16[768,6144]{1,0:T(8,128)(2,1)}) %all-gather.7.cloned.1.call-update) | async-done | bytes 9437200 | tf_op jit(solution)/shard_map/all_gather | solution.py:97
  235.9 11.6 %multiply_reduce_fusion = (f32[768]{0:T(1024)S(1)}, bf16[1,768,576]{1,2,0:T(8,128)(2,1)}) fusion(bf16[1,768,576]{1,2,0:T(8,128)(2,1)} %param.22, f32[768]{0:T(1024)S(1)} %convert_element_type.83, bf16[768,6144]{1,0:T(8,128)(2,1)} %all-gather.7.cloned.1.call-done, bf16[1,576,6144]{2,1,0:T(8,128)(2,1)} %param.23), kind=kOutput, calls=%fused_computation.12 | convolution fusion | flops 5438028800 | bytes 18290688 | tf_op jit(solution)/shard_map/dot_general | solution.py:99
  247.5 31.2 %all-reduce.1 = f32[768]{0:T(1024)S(1)} all-reduce(f32[768]{0:T(1024)S(1)} %get-tuple-element.206), channel_id=4, replica_groups=mesh['seq'=16,'exp'=8] {'seq'}, use_global_device_ids=true, to_apply=%region_9.10.clone | all-reduce | flops 768 | bytes 6144
  278.6 0.2 convolution_bitcast_fusion.6
  278.9 20.6 %psum.7 = f32[128,2]{0,1:T(2,128)} all-reduce(f32[128,2]{0,1:T(2,128)S(1)} %broadcast_select_fusion), channel_id=1, replica_groups=mesh['seq'=16,'exp'=8] {'exp'}, use_global_device_ids=true, to_apply=%region_10.11 | all-reduce | flops 256 | bytes 2048 | tf_op jit(solution)/shard_map/psum | solution.py:114
  299.4 11.9 %fusion.3 = bf16[1,576,6144]{2,1,0:T(8,128)(2,1)} fusion(bf16[768,6144]{1,0:T(8,128)(2,1)} %all-gather.7.cloned.1.call-done, f32[768]{0:T(1024)S(1)} %convert_element_type.83, bf16[1,768,576]{1,2,0:T(8,128)(2,1)S(1)} %copy-done.4), kind=kOutput, calls=%fused_computation.8 | convolution fusion | flops 5453512704 | bytes 17402880 | tf_op jit(solution)/shard_map/dot_general | solution.py:107
  (37 shorter events, 0.5 us)
Async XLA Ops:
  7.2 2.3 copy-start
  7.2 38.9 %copy-start.1 = (u32[128]{0:T(128)S(1)}, u32[128]{0:T(128)}, u32[]{:S(2)}) copy-start(u32[128]{0:T(128)} %constant.81) | copy-start | bytes 1540
  7.2 16.6 %copy-start.3 = (bf16[128,2]{0,1:T(2,128)(2,1)S(1)}, bf16[128,2]{0,1:T(2,128)(2,1)}, u32[]{:S(2)}) copy-start(bf16[128,2]{0,1:T(2,128)(2,1)} %param.20) | copy-start | bytes 1540
  7.2 16.6 %copy-start.2 = (s32[128,2]{0,1:T(2,128)S(1)}, s32[128,2]{0,1:T(2,128)}, u32[]{:S(2)}) copy-start(s32[128,2]{0,1:T(2,128)} %param.21) | copy-start | bytes 3076
  7.2 89.1 %all-gather.9.cloned.1.call-start = ((), (), s32[]{:S(2)}) async-start(), calls=%async_computation.2 | async-start | bytes 8912896 | tf_op jit(solution)/shard_map/all_gather | solution.py:13
  10.7 147.1 %all-gather.11.cloned.1.call-start = ((), (), s32[]{:S(2)}) async-start(), calls=%async_computation.3 | async-start | bytes 8912896 | tf_op jit(solution)/shard_map/all_gather | solution.py:13
  17.0 27.5 %all-to-all-start = ((bf16[8,128,768]{1,2,0:T(8,128)(2,1)}), bf16[8,128,768]{1,2,0:T(8,128)(2,1)S(1)}, u32[]{:S(2)}, u32[]{:S(2)}) async-start(bf16[8,128,768]{1,2,0:T(8,128)(2,1)} %stack.2), calls=%async_computation | async-start | bytes 3145728 | tf_op jit(solution)/shard_map/all_to_all | solution.py:90
  23.8 212.0 %all-gather.7.cloned.1.call-start = ((), (), s32[]{:S(2)}) async-start(), calls=%async_computation.1 | async-start | bytes 10027008 | tf_op jit(solution)/shard_map/all_gather | solution.py:97
  180.3 119.1 %copy-start.4 = (bf16[1,768,576]{1,2,0:T(8,128)(2,1)S(1)}, bf16[1,768,576]{1,2,0:T(8,128)(2,1)}, u32[]{:S(2)}) copy-start(bf16[1,768,576]{1,2,0:T(8,128)(2,1)} %param.22) | copy-start | bytes 2654212
Sparse Core Ops, SparseCore 0:
  10.8 74.4 all-gather.8
  87.5 70.2 all-gather.10
  160.5 75.2 all-gather.6
